TPU v7x, 32 devices: a whole 2x2x4 slice. The times are simulated.
32 devices in a mesh: vocab: 8 (over z, x), dp: 4 (over y, core).
Axes of the slice: x: 2, y: 2, z: 4, core: 2. Of those that a mesh axis runs over, the one named last changes fastest.
Arguments:
- teacher_hidden: bfloat16 [512, 5376], P('dp'), may hold values from -48 to 48
- student_hidden: bfloat16 [512, 2560], P('dp'), may hold values from -48 to 48
- teacher_codes: bfloat16 [16384, 5376], P(('vocab', 'dp')), may hold values from -8 to 7, as said below
- teacher_scales: float32 [16384, 42], P(('vocab', 'dp')), may hold values from 0.003 to 0.07
- student_weight: bfloat16 [16384, 2560], P(('vocab', 'dp')), may hold values from -1 to 1
- loss_scale: bfloat16 [512], P('dp'), may hold values from 2 to 20
Outputs:
- kl: float32 [512], P('dp')
- grad_hidden: bfloat16 [512, 2560], P('dp', 'vocab')
- grad_weight: bfloat16 [16384, 2560], P(('vocab', 'dp'))
Inputs may be any that keep to these rules, and one draw needn't show every extreme that they name: `teacher_codes`: whole numbers.
All inputs are finite; a program needn't handle non-finite values.
Results may differ from a plain program's by a relative error of at most 0.0085.
Values may be sent and summed in bfloat16 or wider, within the bound.
A program may use at most 128 MiB of HBM per device.

v0:
```python
import jax
import jax.numpy as jnp
from jax import lax
from jax.sharding import PartitionSpec as P

GROUP = 128


def dequantize(code_values, scales):
    row_count = code_values.shape[0]
    grouped = code_values.astype(jnp.float32).reshape(row_count, -1, GROUP) * scales[:, :, None]
    return grouped.reshape(row_count, -1).astype(jnp.bfloat16)


def contract_last(left_rows, right_rows):
    return lax.dot_general(
        left_rows, right_rows, (((1,), (1,)), ((), ())), preferred_element_type=jnp.float32
    )


def local(
    teacher_hidden, student_hidden, teacher_codes, teacher_scales, student_weight, loss_scale
):
    tok_rows = teacher_hidden.shape[0]
    teacher_all, student_all, scale_all = (
        lax.all_gather(teacher_hidden, "dp", axis=0, tiled=True),
        lax.all_gather(student_hidden, "dp", axis=0, tiled=True),
        lax.all_gather(loss_scale, "dp", axis=0, tiled=True),
    )
    teacher_table = dequantize(teacher_codes, teacher_scales)
    teacher_logits = contract_last(teacher_all, teacher_table)
    student_logits = contract_last(student_all, student_weight)
    teacher_local = jnp.max(teacher_logits, axis=1)
    student_local = jnp.max(student_logits, axis=1)
    teacher_top, student_top = lax.pmax((teacher_local, student_local), ("vocab", "dp"))
    teacher_exp = jnp.exp(teacher_logits - teacher_top[:, None])
    student_exp = jnp.exp(student_logits - student_top[:, None])
    teacher_total, cross_total, student_total = lax.psum(
        (
            jnp.sum(teacher_exp, axis=1),
            jnp.sum(teacher_exp * (teacher_logits - student_logits), axis=1),
            jnp.sum(student_exp, axis=1),
        ),
        ("vocab", "dp"),
    )
    teacher_lse = teacher_top + jnp.log(teacher_total)
    student_lse = student_top + jnp.log(student_total)
    divergence = cross_total / teacher_total - teacher_lse + student_lse
    own_start = lax.axis_index("dp") * tok_rows
    kl = lax.dynamic_slice_in_dim(divergence, own_start, tok_rows, 0)
    teacher_prob = jnp.exp(teacher_logits - teacher_lse[:, None])
    student_prob = jnp.exp(student_logits - student_lse[:, None])
    logit_grad = (scale_all.astype(jnp.float32)[:, None] * (student_prob - teacher_prob)).astype(
        jnp.bfloat16
    )
    grad_weight = lax.dot_general(
        logit_grad, student_all, (((0,), (0,)), ((), ())), preferred_element_type=jnp.float32
    ).astype(jnp.bfloat16)
    token_part = lax.psum_scatter(
        jnp.dot(logit_grad, student_weight, preferred_element_type=jnp.float32),
        "dp",
        scatter_dimension=0,
        tiled=True,
    )
    grad_hidden = lax.psum_scatter(token_part, "vocab", scatter_dimension=1, tiled=True).astype(
        jnp.bfloat16
    )
    return (kl, grad_hidden, grad_weight)


def solution(mesh):
    in_specs = (
        P("dp", None),
        P("dp", None),
        P(("vocab", "dp"), None),
        P(("vocab", "dp"), None),
        P(("vocab", "dp"), None),
        P("dp"),
    )
    out_specs = (P("dp"), P("dp", "vocab"), P(("vocab", "dp"), None))
    return jax.shard_map(local, mesh=mesh, in_specs=in_specs, out_specs=out_specs, check_vma=False)
```

profile of v0, /device:TPU:0, one launch (start us, length us, event | category | flops | bytes accessed | tf_op | source)
XLA Modules:
  0.0 305.5 jit_solution(14762963266301238189)
XLA Ops:
  7.2 0.0 copy-start
  7.2 0.0 all-gather.6.cloned.1.call-start
  7.2 0.7 all-gather.6.cloned.1.call-update
  7.9 0.0 all-gather.4.cloned.1.call-start
  8.0 0.7 all-gather.4.cloned.1.call-update
  8.7 0.0 copy-start.2
  8.7 0.0 copy-start.1
  8.7 0.0 reduce-scatter.5.cloned.1.call-start
  8.7 8.3 %copy.13 = bf16[512,5376]{0,1:T(8,128)(2,1)} copy(bf16[512,5376]{1,0:T(8,128)(2,1)} %param.8) | data formatting | bytes 11010048 | tf_op args[2]
  17.0 0.0 copy-done.2
  17.0 6.0 %all-gather = bf16[4,1,128]{2,1,0:T(2,128)(2,1)S(1)} all-gather(bf16[1,1,128]{2,1,0:T(2,128)(2,1)S(1)} %bitcast.41), channel_id=1, replica_groups=mesh['vocab'=8,'dp'=4] {'dp'}, dimensions={0}, use_global_device_ids=true | all-gather | bytes 1280 | tf_op jit(solution)/shard_map/all_gather | solution.py:28
  23.0 0.0 copy-done.1
  23.0 6.1 %fusion = bf16[512,5376]{0,1:T(8,128)(2,1)} fusion(bf16[512,5376]{0,1:T(8,128)(2,1)} %copy.13, f32[512,42]{0,1:T(8,128)S(1)} %copy-done.1), kind=kLoop, calls=%fused_computation.1 | loop fusion | flops 8257536 | bytes 11096064 | tf_op jit(solution)/shard_map/convert_element_type | solution.py:12
  29.2 8.7 %all-gather.6.cloned.1.call-done = bf16[512,2560]{1,0:T(8,128)(2,1)} async-done(((bf16[128,2560]{1,0:T(8,128)(2,1)}), bf16[512,2560]{1,0:T(8,128)(2,1)}) %all-gather.6.cloned.1.call-update) | async-done | bytes 2621456 | tf_op jit(solution)/shard_map/all_gather | solution.py:27
  37.8 0.0 copy-done
  37.8 4.3 %fusion.9 = (f32[512]{0:T(512)S(1)}, f32[512,512]{0,1:T(8,128)}) fusion(bf16[512,2560]{1,0:T(8,128)(2,1)} %all-gather.6.cloned.1.call-done, bf16[512,2560]{1,0:T(8,128)(2,1)S(1)} %copy-done), kind=kOutput, calls=%fused_computation.18 | convolution fusion | flops 1342438912 | bytes 6293504 | tf_op jit(solution)/shard_map/dot_general | solution.py:16
  42.1 39.2 %all-gather.4.cloned.1.call-done = bf16[512,5376]{1,0:T(8,128)(2,1)} async-done(((bf16[128,5376]{1,0:T(8,128)(2,1)}), bf16[512,5376]{1,0:T(8,128)(2,1)}) %all-gather.4.cloned.1.call-update) | async-done | bytes 5505040 | tf_op jit(solution)/shard_map/all_gather | solution.py:26
  81.3 8.2 %fusion.10 = (f32[512]{0:T(512)S(1)}, f32[512,512]{1,0:T(8,128)}) fusion(bf16[512,5376]{0,1:T(8,128)(2,1)} %fusion, bf16[512,5376]{1,0:T(8,128)(2,1)} %all-gather.4.cloned.1.call-done), kind=kOutput, calls=%fused_computation.19 | convolution fusion | flops 2818833920 | bytes 12060672 | tf_op jit(solution)/shard_map/dot_general | solution.py:16
  89.6 39.2 %all-reduce.1 = (f32[512]{0:T(512)S(1)}, f32[512]{0:T(512)S(1)}) all-reduce(f32[512]{0:T(512)S(1)} %get-tuple-element.23, f32[512]{0:T(512)S(1)} %get-tuple-element.25), channel_id=1, replica_groups=mesh['vocab'=8,'dp'=4] {'vocab','dp'}, use_global_device_ids=true, to_apply=%region_7.0 | all-reduce | flops 1024 | bytes 8192 | tf_op jit(solution)/shard_map/pmax | solution.py:35
  128.8 1.9 fusion.3
  130.7 41.1 %all-reduce = (f32[512]{0:T(512)S(1)}, f32[512]{0:T(512)S(1)}, f32[512]{0:T(512)S(1)}) all-reduce(f32[512]{0:T(512)S(1)} %get-tuple-element.14, f32[512]{0:T(512)S(1)} %get-tuple-element.13, f32[512]{0:T(512)S(1)} %get-tuple-element.12), channel_id=1, replica_groups=mesh['vocab'=8,'dp'=4] {'vocab','dp'}, use_global_device_ids=true, to_apply=%region_9.0 | all-reduce | flops 1536 | bytes 12288 | tf_op jit(solution)/shard_map/psum | solution.py:38
  171.8 1.8 fusion.7
  173.7 3.9 %fusion.11 = f32[512,2560]{1,0:T(8,128)} fusion(bf16[512,512]{0,1:T(8,128)(2,1)S(1)} %fusion.7, bf16[512,2560]{1,0:T(8,128)(2,1)S(1)} %copy-done), kind=kOutput, calls=%fused_computation.20 | convolution fusion | flops 1342177280 | bytes 8388608 | tf_op jit(solution)/shard_map/dot_general | solution.py:60
  177.5 0.0 reduce-scatter.5.cloned.1.call-update
  177.6 0.0 reduce-scatter.7.cloned.1.call-start
  177.6 51.2 %reduce-scatter.5.cloned.1.call-done = f32[128,2560]{1,0:T(8,128)} async-done(((f32[512,2560]{1,0:T(8,128)}), f32[128,2560]{1,0:T(8,128)}) %reduce-scatter.5.cloned.1.call-update) | async-done | bytes 1310736 | tf_op jit(solution)/shard_map/reduce_scatter | solution.py:59
  228.8 2.8 copy.15
  231.6 0.0 reduce-scatter.7.cloned.1.call-update
  231.6 0.6 dynamic_slice.3
  232.2 4.8 %convolution_convert_fusion = bf16[512,2560]{1,0:T(8,128)(2,1)} fusion(bf16[512,512]{0,1:T(8,128)(2,1)S(1)} %fusion.7, bf16[512,2560]{1,0:T(8,128)(2,1)} %all-gather.6.cloned.1.call-done), kind=kOutput, calls=%fused_computation.2 | convolution fusion | flops 1343488000 | bytes 5767168 | tf_op jit(solution)/shard_map/dot_general | solution.py:56
  236.9 60.3 %reduce-scatter.7.cloned.1.call-done = f32[320,128]{1,0:T(8,128)} async-done(((f32[2560,128]{1,0:T(8,128)}), f32[320,128]{1,0:T(8,128)}) %reduce-scatter.7.cloned.1.call-update) | async-done | bytes 163856
  297.2 1.0 copy.16
  298.2 0.8 copy.14
  (2 shorter events, 0.0 us)
Async XLA Ops:
  7.2 30.7 %copy-start = (bf16[512,2560]{1,0:T(8,128)(2,1)S(1)}, bf16[512,2560]{1,0:T(8,128)(2,1)}, u32[]{:S(2)}) copy-start(bf16[512,2560]{1,0:T(8,128)(2,1)} %param.10) | copy-start | bytes 7864324
  7.2 30.7 %all-gather.6.cloned.1.call-start = ((), (), s32[]{:S(2)}) async-start(), calls=%async_computation.3 | async-start | bytes 3276800 | tf_op jit(solution)/shard_map/all_gather | solution.py:27
  7.9 73.4 %all-gather.4.cloned.1.call-start = ((), (), s32[]{:S(2)}) async-start(), calls=%async_computation.2 | async-start | bytes 6881280 | tf_op jit(solution)/shard_map/all_gather | solution.py:26
  8.7 8.3 %copy-start.2 = (bf16[128]{0:T(256)(128)(2,1)S(1)}, bf16[128]{0:T(256)(128)(2,1)}, u32[]{:S(2)}) copy-start(bf16[128]{0:T(256)(128)(2,1)} %param.11) | copy-start | bytes 772
  8.7 14.4 %copy-start.1 = (f32[512,42]{0,1:T(8,128)S(1)}, f32[512,42]{0,1:T(8,128)}, u32[]{:S(2)}) copy-start(f32[512,42]{0,1:T(8,128)} %param.9) | copy-start | bytes 258052
  8.7 220.1 %reduce-scatter.5.cloned.1.call-start = ((), (), s32[]{:S(2)}) async-start(), calls=%async_computation.4 | async-start | bytes 6553600 | tf_op jit(solution)/shard_map/reduce_scatter | solution.py:59
  177.6 119.7 %reduce-scatter.7.cloned.1.call-start = ((), (), s32[]{:S(2)}) async-start(), calls=%async_computation.5 | async-start | bytes 1474560
Sparse Core Ops, SparseCore 0:
  9.5 28.2 all-gather.5
  39.4 41.8 all-gather.3
  177.7 51.0 reduce-scatter.4
  232.0 65.1 reduce-scatter.6
where the time goes:
time: 306 us
  waiting for transfers between devices  161 us (53%)
  blocking collectives  86.3 us (28%)
  matrix products  21.1 us (7%)
  between operations  13.8 us (5%)
  local copies, waits for them, and re-layouts  13.4 us (4%)
  other arithmetic  9.94 us (3%)
    unnamed x5, waiting for transfers between devices  61.7 us
    reduce_scatter x1, waiting for transfers between devices, local(): lax.psum_scatter(jnp.dot(logit_grad, student_weight, preferred_element_ty...  51.2 us
    psum x1, blocking collectives, local(): lax.psum((jnp.sum(teacher_exp, axis=1), jnp.sum(teacher_exp * (teacher_lo...  41.1 us
    pmax x1, blocking collectives, local(): lax.pmax((teacher_local, student_local), ('vocab', 'dp'))  39.2 us
    all_gather x1, waiting for transfers between devices, local(): lax.all_gather(teacher_hidden, 'dp', axis=0, tiled=True)  39.2 us
    unnamed x10, local copies, waits for them, and re-layouts  12.9 us
    dot_general x2, matrix products, contract_last(): lax.dot_general(left_rows, right_rows, (((1,), (1,)), ((), ())), preferre...  12.5 us
    all_gather x1, waiting for transfers between devices, local(): lax.all_gather(student_hidden, 'dp', axis=0, tiled=True)  8.66 us
  transfers between devices with their start and end apart: 4, of which 4 were waited for; matrix products, arithmetic and copies ran while one was open for 8% of the time, Pallas kernels for 0%

commit v1 on v0

--- a/solution.py
+++ b/solution.py
@@ -4,6 +4,13 @@
 from jax.sharding import PartitionSpec as P
 
 GROUP = 128
+
+
+def exchange_gather(block, axis, dim):
+    size = lax.axis_size(axis)
+    parts = jnp.stack([block for _ in range(size)])
+    parts = lax.all_to_all(parts, axis, split_axis=0, concat_axis=0)
+    return jnp.concatenate(parts, axis=dim)
 
 
 def dequantize(code_values, scales):
@@ -23,7 +30,7 @@
 ):
     tok_rows = teacher_hidden.shape[0]
     teacher_all, student_all, scale_all = (
-        lax.all_gather(teacher_hidden, "dp", axis=0, tiled=True),
+        exchange_gather(teacher_hidden, "dp", 0),
         lax.all_gather(student_hidden, "dp", axis=0, tiled=True),
         lax.all_gather(loss_scale, "dp", axis=0, tiled=True),
     )

time: 306 us -> 340 us (1.11)
  blocking collectives: 86.3 us -> 159 us
  waiting for transfers between devices: 161 us -> 112 us
  starting transfers between devices: 0.16 us -> 5.34 us
  local copies, waits for them, and re-layouts: 13.4 us -> 17.7 us
    all_gather x1, blocking collectives: 6.02 us -> 77.7 us  [local(): lax.all_gather(loss_scale, 'dp', axis=0, tiled=True)]
    all_gather x1 -> x0, waiting for transfers between devices: 39.2 us -> none  [local(): lax.all_gather(teacher_hidden, 'dp', axis=0, tiled=True)]
    all_gather x1, waiting for transfers between devices: 8.66 us -> 0.01 us  [local(): lax.all_gather(student_hidden, 'dp', axis=0, tiled=True)]
    all_to_all x0 -> x1, starting transfers between devices: none -> 5.22 us  [exchange_gather(): parts = lax.all_to_all(parts, axis, split_axis=0, concat_axis=0)]
    another operation x0 -> x1, local copies, waits for them, and re-layouts: none -> 4.19 us  [exchange_gather(): parts = jnp.stack([block for _ in range(size)])]
    unnamed x5 -> x4, waiting for transfers between devices: 61.7 us -> 61 us
  transfers between devices with their start and end apart: 4 -> 4, of which waited for: 4 -> 2; matrix products, arithmetic and copies ran while one was open for 8% -> 8% of each run, Pallas kernels for 0% -> 0%
where the time goes in v1:
time: 340 us; the launch traced here: 339 us
  blocking collectives  159 us (47%)
  waiting for transfers between devices  112 us (33%)
  matrix products  21.1 us (6%)
  local copies, waits for them, and re-layouts  17.7 us (5%)
  between operations  13.8 us (4%)
  other arithmetic  9.84 us (3%)
  starting transfers between devices  5.34 us (2%)
    all_gather x1, blocking collectives, local(): lax.all_gather(loss_scale, 'dp', axis=0, tiled=True)  77.7 us
    unnamed x4, waiting for transfers between devices  61 us
    reduce_scatter x1, waiting for transfers between devices, local(): lax.psum_scatter(jnp.dot(logit_grad, student_weight, preferred_element_ty...  51.2 us
    psum x1, blocking collectives, local(): lax.psum((jnp.sum(teacher_exp, axis=1), jnp.sum(teacher_exp * (teacher_lo...  41 us
    pmax x1, blocking collectives, local(): lax.pmax((teacher_local, student_local), ('vocab', 'dp'))  40.2 us
    unnamed x10, local copies, waits for them, and re-layouts  12.9 us
    dot_general x2, matrix products, contract_last(): lax.dot_general(left_rows, right_rows, (((1,), (1,)), ((), ())), preferre...  12.5 us
  transfers between devices with their start and end apart: 4, of which 2 were waited for; matrix products, arithmetic and copies ran while one was open for 8% of the time, Pallas kernels for 0%

profile of v1, /device:TPU:0, one launch (start us, length us, event | category | flops | bytes accessed | tf_op | source)
XLA Modules:
  0.0 339.1 jit_solution(4366638004036172114)
XLA Ops:
  7.2 0.0 copy-start
  7.2 0.0 all-gather.3.cloned.1.call-start
  7.2 0.7 all-gather.3.cloned.1.call-update
  7.9 4.2 %stack.2 = bf16[4,128,5376]{2,1,0:T(8,128)(2,1)} broadcast(bf16[128,5376]{1,0:T(8,128)(2,1)} %param.6), dimensions={1,2} | broadcast | bytes 6881280 | tf_op jit(solution)/shard_map/stack | solution.py:11
  12.1 0.0 copy-start.2
  12.1 5.2 %all-to-all-start = ((bf16[4,128,5376]{2,1,0:T(8,128)(2,1)}), bf16[4,128,5376]{2,1,0:T(8,128)(2,1)}, u32[]{:S(2)}, u32[]{:S(2)}) async-start(bf16[4,128,5376]{2,1,0:T(8,128)(2,1)} %stack.2), calls=%async_computation | async-start | bytes 11010048 | tf_op jit(solution)/shard_map/all_to_all | solution.py:12
  17.3 0.0 reduce-scatter.5.cloned.1.call-start
  17.4 0.0 copy-done.2
  17.4 77.7 %all-gather = bf16[4,1,128]{2,1,0:T(2,128)(2,1)S(1)} all-gather(bf16[1,1,128]{2,1,0:T(2,128)(2,1)S(1)} %bitcast.42), channel_id=1, replica_groups=mesh['vocab'=8,'dp'=4] {'dp'}, dimensions={0}, use_global_device_ids=true | all-gather | bytes 1280 | tf_op jit(solution)/shard_map/all_gather | solution.py:35
  95.1 0.0 copy-start.1
  95.1 8.4 %copy.13 = bf16[512,5376]{0,1:T(8,128)(2,1)} copy(bf16[512,5376]{1,0:T(8,128)(2,1)} %param.8) | data formatting | bytes 11010048 | tf_op args[2]
  103.5 0.0 copy-done.1
  103.5 6.0 %fusion = bf16[512,5376]{0,1:T(8,128)(2,1)} fusion(bf16[512,5376]{0,1:T(8,128)(2,1)} %copy.13, f32[512,42]{0,1:T(8,128)S(1)} %copy-done.1), kind=kLoop, calls=%fused_computation.1 | loop fusion | flops 8257536 | bytes 11096064 | tf_op jit(solution)/shard_map/convert_element_type | solution.py:19
  109.5 0.0 all-gather.3.cloned.1.call-done
  109.5 0.0 copy-done
  109.5 4.3 %fusion.9 = (f32[512]{0:T(512)S(1)}, f32[512,512]{0,1:T(8,128)}) fusion(bf16[512,2560]{1,0:T(8,128)(2,1)} %all-gather.3.cloned.1.call-done, bf16[512,2560]{1,0:T(8,128)(2,1)S(1)} %copy-done), kind=kOutput, calls=%fused_computation.18 | convolution fusion | flops 1342438912 | bytes 6293504 | tf_op jit(solution)/shard_map/dot_general | solution.py:23
  113.8 0.0 all-to-all-done
  113.8 8.3 %fusion.10 = (f32[512]{0:T(512)S(1)}, f32[512,512]{1,0:T(8,128)}) fusion(bf16[512,5376]{0,1:T(8,128)(2,1)} %fusion, bf16[512,5376]{1,0:T(8,128)(2,1)} %bitcast.1), kind=kOutput, calls=%fused_computation.19 | convolution fusion | flops 2818833920 | bytes 12060672 | tf_op jit(solution)/shard_map/dot_general | solution.py:23
  122.1 40.2 %all-reduce.1 = (f32[512]{0:T(512)S(1)}, f32[512]{0:T(512)S(1)}) all-reduce(f32[512]{0:T(512)S(1)} %get-tuple-element.23, f32[512]{0:T(512)S(1)} %get-tuple-element.25), channel_id=1, replica_groups=mesh['vocab'=8,'dp'=4] {'vocab','dp'}, use_global_device_ids=true, to_apply=%region_7.0 | all-reduce | flops 1024 | bytes 8192 | tf_op jit(solution)/shard_map/pmax | solution.py:42
  162.3 1.9 fusion.3
  164.2 41.0 %all-reduce = (f32[512]{0:T(512)S(1)}, f32[512]{0:T(512)S(1)}, f32[512]{0:T(512)S(1)}) all-reduce(f32[512]{0:T(512)S(1)} %get-tuple-element.14, f32[512]{0:T(512)S(1)} %get-tuple-element.13, f32[512]{0:T(512)S(1)} %get-tuple-element.12), channel_id=1, replica_groups=mesh['vocab'=8,'dp'=4] {'vocab','dp'}, use_global_device_ids=true, to_apply=%region_9.0 | all-reduce | flops 1536 | bytes 12288 | tf_op jit(solution)/shard_map/psum | solution.py:45
  205.3 1.8 fusion.7
  207.1 3.9 %fusion.11 = f32[512,2560]{1,0:T(8,128)} fusion(bf16[512,512]{0,1:T(8,128)(2,1)S(1)} %fusion.7, bf16[512,2560]{1,0:T(8,128)(2,1)S(1)} %copy-done), kind=kOutput, calls=%fused_computation.20 | convolution fusion | flops 1342177280 | bytes 8388608 | tf_op jit(solution)/shard_map/dot_general | solution.py:67
  211.0 0.0 reduce-scatter.5.cloned.1.call-update
  211.0 0.0 reduce-scatter.7.cloned.1.call-start
  211.1 51.2 %reduce-scatter.5.cloned.1.call-done = f32[128,2560]{1,0:T(8,128)} async-done(((f32[512,2560]{1,0:T(8,128)}), f32[128,2560]{1,0:T(8,128)}) %reduce-scatter.5.cloned.1.call-update) | async-done | bytes 1310736 | tf_op jit(solution)/shard_map/reduce_scatter | solution.py:66
  262.3 2.8 copy.15
  265.1 0.0 reduce-scatter.7.cloned.1.call-update
  265.1 0.6 dynamic_slice.3
  265.7 4.8 %convolution_convert_fusion = bf16[512,2560]{1,0:T(8,128)(2,1)} fusion(bf16[512,512]{0,1:T(8,128)(2,1)S(1)} %fusion.7, bf16[512,2560]{1,0:T(8,128)(2,1)} %all-gather.3.cloned.1.call-done), kind=kOutput, calls=%fused_computation.2 | convolution fusion | flops 1343488000 | bytes 5767168 | tf_op jit(solution)/shard_map/dot_general | solution.py:63
  270.5 60.3 %reduce-scatter.7.cloned.1.call-done = f32[320,128]{1,0:T(8,128)} async-done(((f32[2560,128]{1,0:T(8,128)}), f32[320,128]{1,0:T(8,128)}) %reduce-scatter.7.cloned.1.call-update) | async-done | bytes 163856
  330.7 1.0 copy.16
  331.8 0.8 copy.14
  (2 shorter events, 0.0 us)
Async XLA Ops:
  7.2 102.4 %copy-start = (bf16[512,2560]{1,0:T(8,128)(2,1)S(1)}, bf16[512,2560]{1,0:T(8,128)(2,1)}, u32[]{:S(2)}) copy-start(bf16[512,2560]{1,0:T(8,128)(2,1)} %param.10) | copy-start | bytes 7864324
  7.2 102.4 %all-gather.3.cloned.1.call-start = ((), (), s32[]{:S(2)}) async-start(), calls=%async_computation.3 | async-start | bytes 3276800 | tf_op jit(solution)/shard_map/all_gather | solution.py:34
  12.1 5.3 %copy-start.2 = (bf16[128]{0:T(256)(128)(2,1)S(1)}, bf16[128]{0:T(256)(128)(2,1)}, u32[]{:S(2)}) copy-start(bf16[128]{0:T(256)(128)(2,1)} %param.11) | copy-start | bytes 772
  12.1 101.7 %all-to-all-start = ((bf16[4,128,5376]{2,1,0:T(8,128)(2,1)}), bf16[4,128,5376]{2,1,0:T(8,128)(2,1)}, u32[]{:S(2)}, u32[]{:S(2)}) async-start(bf16[4,128,5376]{2,1,0:T(8,128)(2,1)} %stack.2), calls=%async_computation | async-start | bytes 11010048 | tf_op jit(solution)/shard_map/all_to_all | solution.py:12
  17.3 245.0 %reduce-scatter.5.cloned.1.call-start = ((), (), s32[]{:S(2)}) async-start(), calls=%async_computation.4 | async-start | bytes 6553600 | tf_op jit(solution)/shard_map/reduce_scatter | solution.py:66
  95.1 8.4 %copy-start.1 = (f32[512,42]{0,1:T(8,128)S(1)}, f32[512,42]{0,1:T(8,128)}, u32[]{:S(2)}) copy-start(f32[512,42]{0,1:T(8,128)} %param.9) | copy-start | bytes 258052
  211.0 119.7 %reduce-scatter.7.cloned.1.call-start = ((), (), s32[]{:S(2)}) async-start(), calls=%async_computation.5 | async-start | bytes 1474560
Sparse Core Ops, SparseCore 0:
  9.5 42.3 all-gather.2
  211.1 51.1 reduce-scatter.4
  265.7 64.9 reduce-scatter.6
